TPU v7x, 128 devices: a whole 4x4x4 slice. The times are simulated.
128 devices in a mesh: group: 4 (over x), shard: 32 (over z, y, core).
Axes of the slice: x: 4, y: 4, z: 4, core: 2. Of those that a mesh axis runs over, the one named last changes fastest.
Arguments:
- samples: bfloat16 [16384, 1, 4096], P(('group', 'shard')), may hold values from -6 to 6
- fan_taps: float32 [33, 2048], replicated, may hold values from -1 to 1
- pair_blocks: int32 [512, 2], replicated, may hold values from 0 to 127
- pair_valid: int32 [512], P(('group', 'shard')), may hold values 0 or 1
- coil_offsets: int32 [128], replicated, may hold values from 0 to 63
Outputs:
- correlations: float32 [512, 128, 512], P(('group', 'shard'))
Inputs may be any that keep to these rules, and one draw needn't show every extreme that they name: `pair_blocks`: block indices.
All inputs are finite; a program needn't handle non-finite values. No bound on the sum of `pair_valid` on one device may be relied on, other than what follows from the above.
Results may differ from a plain program's by a relative error of at most 0.0076.
Values may be sent and summed in bfloat16 or wider, within the bound.
A program may use at most 192 MiB of HBM per device.

v0:
```python
import jax
import jax.numpy as jnp
from jax import lax
from jax.sharding import PartitionSpec as P

HALF = 16
SMOOTH = 64
NLAG = 512
EPSILON = 1e-05


def with_halo(cells, sides, width):
    for axis, dim in sides:
        count = lax.axis_size(axis)
        ends = count - 1
        head = lax.slice_in_dim(cells, 0, width, axis=dim)
        tail = lax.slice_in_dim(cells, cells.shape[dim] - width, cells.shape[dim], axis=dim)
        cells = jnp.concatenate(
            [
                lax.ppermute(tail, axis, [(i, (i + 1) % count) for i in range(ends)]),
                cells,
                lax.ppermute(head, axis, [((i + 1) % count, i) for i in range(ends)]),
            ],
            axis=dim,
        )
    return cells


def forward_tables(length, bin_count):
    split = 1 << length.bit_length() // 2
    coarse_n = (jnp.arange(length // split, dtype=jnp.int32) * split)[:, None]
    fine_n = jnp.arange(split, dtype=jnp.int32)[:, None]
    cols_k = jnp.arange(bin_count, dtype=jnp.int32)[None, :]
    coarse_ph = jnp.mod(coarse_n * cols_k, length).astype(jnp.float32) * (2.0 * jnp.pi / length)
    fine_ph = jnp.mod(fine_n * cols_k, length).astype(jnp.float32) * (2.0 * jnp.pi / length)
    cos_a = jnp.cos(coarse_ph)[:, None, :]
    sin_a = jnp.sin(coarse_ph)[:, None, :]
    cos_b = jnp.cos(fine_ph)[None, :, :]
    sin_b = jnp.sin(fine_ph)[None, :, :]
    cosine = (cos_a * cos_b - sin_a * sin_b).reshape(length, bin_count)
    sine_vals = (sin_a * cos_b + cos_a * sin_b).reshape(length, bin_count)
    scaled = 1.0 / jnp.sqrt(jnp.float32(length))
    return (jnp.concatenate([cosine, -sine_vals], axis=1) * scaled).astype(jnp.bfloat16)


def inverse_tables(length, bin_count, lag_count):
    freq_index = jnp.arange(bin_count, dtype=jnp.int32)[:, None]
    lagged = jnp.arange(lag_count, dtype=jnp.int32)[None, :] - lag_count // 2
    phases = jnp.mod(freq_index * lagged, length).astype(jnp.float32) * (2.0 * jnp.pi / length)
    return jnp.stack([jnp.cos(phases), -jnp.sin(phases)]).astype(jnp.bfloat16)


def box_mean(power_sum):
    bin_count = power_sum.shape[1]
    zero_row = jnp.zeros_like(power_sum[:, :1])
    prefix = jnp.concatenate([zero_row, jnp.cumsum(power_sum, axis=1)], axis=1)
    last_row = prefix[:, bin_count : bin_count + 1]
    first_row = prefix[:, 0:1]
    upper_vals = jnp.concatenate(
        [
            prefix[:, SMOOTH + 1 :],
            jnp.broadcast_to(last_row, (prefix.shape[0], SMOOTH) + prefix.shape[2:]),
        ],
        axis=1,
    )
    lower_vals = jnp.concatenate(
        [
            jnp.broadcast_to(first_row, (prefix.shape[0], SMOOTH + 1) + prefix.shape[2:]),
            prefix[:, 1 : bin_count - SMOOTH],
        ],
        axis=1,
    )
    bins_k = jnp.arange(bin_count, dtype=jnp.int32)
    counts = (
        jnp.minimum(bins_k + SMOOTH, bin_count - 1) - jnp.maximum(bins_k - SMOOTH, 0) + 1
    ).astype(jnp.float32)
    return (upper_vals - lower_vals) / counts[None, :, None]


def whiten(padded, fan_taps):
    width = padded.shape[3] - 2 * HALF
    filtered = jnp.zeros(padded.shape[:3] + (width,), jnp.float32)
    for offset in range(2 * HALF + 1):
        filtered = filtered + fan_taps[offset][None, None, :, None] * padded[
            :, :, :, offset : offset + width
        ].astype(jnp.float32)
    power_sum = filtered[:, 0] * filtered[:, 0] + filtered[:, 1] * filtered[:, 1]
    mean_power = box_mean(power_sum)
    return (filtered * lax.rsqrt(mean_power + EPSILON)[:, None]).astype(jnp.bfloat16)


def body(samples, fan_taps, pair_blocks, pair_valid, coil_offsets):
    block_width = samples.shape[0]
    segments = samples.shape[1]
    length = samples.shape[2]
    bin_count = length // 2
    groups = lax.axis_size("group")
    shards = lax.axis_size("shard")
    devices = groups * shards
    bins_device = bin_count // devices
    forward = forward_tables(length, bin_count)
    spectra = jnp.einsum("cst,tk->skc", samples, forward, preferred_element_type=jnp.float32)
    padded = with_halo(
        spectra.astype(jnp.bfloat16).reshape(segments, 2, bin_count, samples.shape[0]),
        ((("group", "shard"), 3),),
        HALF,
    )
    whitened = whiten(padded, fan_taps)
    banded = lax.all_to_all(whitened, ("group", "shard"), split_axis=2, concat_axis=3, tiled=True)
    first_block = pair_blocks[:, 0]
    second_block = pair_blocks[:, 1]
    blocks = banded.reshape(segments, 2, bins_device, devices, block_width)
    rolled = jnp.roll(blocks, -(block_width // 2), axis=4)
    left_side = jnp.take(blocks, first_block, axis=3)
    right_side = jnp.take(rolled, second_block, axis=3)
    form = "skpc,skpc->kpc"
    real_part = jnp.einsum(
        form, left_side[:, 0], right_side[:, 0], preferred_element_type=jnp.float32
    ) + jnp.einsum(form, left_side[:, 1], right_side[:, 1], preferred_element_type=jnp.float32)
    imag_part = jnp.einsum(
        form, left_side[:, 1], right_side[:, 0], preferred_element_type=jnp.float32
    ) - jnp.einsum(form, left_side[:, 0], right_side[:, 1], preferred_element_type=jnp.float32)
    block_ids = jnp.arange(devices, dtype=jnp.int32)[None, :]
    first_offset = jnp.sum(
        jnp.where(first_block[:, None] == block_ids, coil_offsets[None, :], 0), axis=1
    )
    second_offset = jnp.sum(
        jnp.where(second_block[:, None] == block_ids, coil_offsets[None, :], 0), axis=1
    )
    shift_samples = first_offset - second_offset
    bin_index = lax.axis_index(("group", "shard")) * bins_device + jnp.arange(
        bins_device, dtype=jnp.int32
    )
    phases = jnp.mod(bin_index[:, None] * shift_samples[None, :], length).astype(jnp.float32) * (
        2.0 * jnp.pi / length
    )
    cosine = jnp.cos(phases)[:, :, None]
    sine_values = jnp.sin(phases)[:, :, None]
    cross_spec = jnp.stack(
        [real_part * cosine + imag_part * sine_values, imag_part * cosine - real_part * sine_values]
    ).astype(jnp.bfloat16)
    owned_spec = lax.all_to_all(
        cross_spec, ("group", "shard"), split_axis=2, concat_axis=1, tiled=True
    )
    inverse = inverse_tables(length, bin_count, NLAG)
    correlations = jnp.einsum(
        "rkpc,rkl->pcl", owned_spec, inverse, preferred_element_type=jnp.float32
    )
    weights = pair_valid.astype(jnp.float32) / jnp.sqrt(jnp.float32(bin_count * segments))
    return correlations * weights[:, None, None]


def solution(mesh):
    return jax.shard_map(
        body,
        mesh=mesh,
        in_specs=(P(("group", "shard"), None, None), P(), P(), P(("group", "shard")), P()),
        out_specs=P(("group", "shard"), None, None),
        check_vma=False,
    )
```

profile of v0, /device:TPU:1, one launch (start us, length us, event | category | flops | bytes accessed | tf_op | source)
XLA Modules:
  0.0 236.7 jit_solution(15228262035999444965)
XLA Ops:
  0.0 2.0 fusion.74
  2.1 2.1 fusion.77
  4.2 22.0 %multiply_subtract_fusion = (f32[64,64,2048]{2,1,0:T(8,128)}, f32[64,64,2048]{2,1,0:T(8,128)}) fusion(f32[64,2048]{1,0:T(8,128)S(1)} %get-tuple-element.57, f32[64,2048]{1,0:T(8,128)S(1)} %get-tuple-element.56, f32[64,2048]{1,0:T(8,128)S(1)} %get-tuple-element.58, f32[64,2048]{1,0:T(8,128)S(1)} %get-tuple-element.55), kind=kLoop, calls=%fused_computation.5 | loop fusion | flops 58720256 | bytes 69206016 | tf_op jit(solution)/shard_map/sub | solution.py:40
  26.2 22.9 %fusion.3 = bf16[4096,128]{1,0:T(8,128)(2,1)S(1)} fusion(f32[4096,2048]{1,0:T(8,128)} %bitcast.155, f32[4096,2048]{1,0:T(8,128)} %bitcast.154, bf16[128,1,4096]{2,0,1:T(8,128)(2,1)S(1)} %copy-done), kind=kOutput, calls=%fused_computation.76 | convolution fusion | flops 4345823232 | bytes 69206016 | tf_op jit(solution)/shard_map/cst,tk->skc/dot_general | solution.py:102
  49.1 0.0 copy-start.3
  49.2 0.4 fusion.92
  49.5 0.6 copy-done.3
  50.1 0.3 copy.61
  50.4 4.6 %collective-permute-start = (bf16[1,2,2048,16]{2,3,1,0:T(8,128)(2,1)S(1)}, bf16[1,2,2048,16]{2,3,1,0:T(8,128)(2,1)S(1)}, u32[]{:S(2)}, u32[]{:S(2)}) collective-permute-start(bf16[1,2,2048,16]{2,3,1,0:T(8,128)(2,1)S(1)} %copy.61), channel_id=1, source_target_pairs={{0,1},{1,2},{2,3},{3,4},{4,5},{5,6},{6,7},{7,8},{8,9},{9,10},{10,1... | collective-permute-start | bytes 393224 | tf_op jit(solution)/shard_map/ppermute | solution.py:20
  55.0 0.3 copy.63
  55.3 2.2 collective-permute-start.1
  57.6 0.0 copy-done.7
  57.6 0.7 fusion.93
  58.3 0.7 fusion.94
  59.1 0.0 copy-start.17
  59.1 0.0 copy-start.19
  59.2 0.4 select_reduce_fusion
  59.5 0.2 copy-done.17
  59.7 0.2 fusion.82
  59.9 0.1 copy.72
  60.1 0.9 copy.75
  60.9 0.6 fusion.86
  61.5 0.0 collective-permute-done
  61.5 1.3 copy.62
  62.9 0.0 collective-permute-done.1
  62.9 1.3 copy.64
  64.2 0.0 copy-done.10
  64.2 0.0 copy-done.11
  64.2 0.0 copy-done.12
  64.2 0.0 copy-done.13
  64.2 0.0 copy-done.14
  64.2 0.0 copy-done.15
  64.3 40.0 %multiply_add_fusion = f32[1,2,2048,128]{3,2,1,0:T(8,128)S(1)} fusion(bf16[1,2,2048,128]{3,2,1,0:T(8,128)(2,1)S(1)} %bitcast.157, bf16[1,2,2048,16]{3,2,1,0:T(8,128)(2,1)} %copy.64, bf16[1,2,2048,16]{3,2,1,0:T(8,128)(2,1)} %copy.62, f32[2048]{0:T(1024)} %bitcast.194, f32[2048]{0:T(1024)} %bitcast.195, f32[2048]{0:T(1024)S(1)} %bitcast.164, ...), kind=kLoop, calls=%fused_computation.103 | loop fusion | flops 101711872 | bytes 3678208 | tf_op jit(solution)/shard_map/add | solution.py:84
  104.2 0.1 fusion.54
  104.3 0.6 fusion.60
  105.0 1.3 copy.66
  106.3 1.3 bitcast_add_fusion
  107.6 0.1 slice.438
  107.7 0.1 slice.440
  107.8 0.5 copy-done.16
  108.3 0.4 fusion.58
  108.7 0.2 multiply_convert_fusion
  108.9 9.5 %copy.67 = bf16[1,2,2048,128]{3,1,0,2:T(2,128)(2,1)} copy(bf16[1,2,2048,128]{3,2,1,0:T(8,128)(2,1)S(1)} %multiply_convert_fusion) | data formatting | bytes 2097152 | tf_op jit(solution)/shard_map/convert_element_type | solution.py:89
  118.3 11.2 %all-to-all-start = ((bf16[1,2,2048,128]{3,1,0,2:T(2,128)(2,1)}), bf16[1,2,2048,128]{3,1,0,2:T(2,128)(2,1)S(1)}, u32[]{:S(2)}, u32[]{:S(2)}) async-start(bf16[1,2,2048,128]{3,1,0,2:T(2,128)(2,1)} %copy.67), calls=%async_computation | async-start | bytes 2097152 | tf_op jit(solution)/shard_map/all_to_all | solution.py:109
  129.5 0.0 copy-done.20
  129.6 19.0 %all-to-all-done = bf16[1,2,2048,128]{3,1,0,2:T(2,128)(2,1)S(1)} async-done(((bf16[1,2,2048,128]{3,1,0,2:T(2,128)(2,1)}), bf16[1,2,2048,128]{3,1,0,2:T(2,128)(2,1)S(1)}, u32[]{:S(2)}, u32[]{:S(2)}) %all-to-all-start) | async-done | bytes 1048608 | tf_op jit(solution)/shard_map/all_to_all | solution.py:109
  148.6 0.1 copy.68
  148.7 0.5 fusion.91
  149.2 0.6 maximum_bitcast_fusion.6
  149.8 3.5 %gather_fusion.1 = bf16[512,2,16,128]{3,2,1,0:T(8,128)(2,1)} fusion(bf16[2,16,128,128]{3,1,2,0:T(8,128)(2,1)S(1)} %maximum_bitcast_fusion.6, s32[1024]{0:T(1024)S(1)} %pad_clamp_fusion), kind=kCustom, calls=%fused_computation.1.clone | custom fusion | bytes 8390656 | tf_op jit(solution)/shard_map/jit(_take)/gather | solution.py:115
  153.3 4.6 %bitcast_select_fusion = bf16[1,2,16,512,128]{4,2,3,1,0:T(8,128)(2,1)} fusion(bf16[512,2,16,128]{3,2,1,0:T(8,128)(2,1)} %gather_fusion.1, pred[512]{0:T(512)(128)(4,1)S(1)} %compare_and_fusion), kind=kLoop, calls=%fused_computation.90 | loop fusion | flops 2097152 | bytes 8389120 | tf_op jit(solution)/shard_map/jit(_take)/select_n | solution.py:115
  157.9 3.5 %gather_fusion = bf16[512,2,16,128]{3,2,1,0:T(8,128)(2,1)} fusion(bf16[2,16,128,128]{3,1,2,0:T(8,128)(2,1)S(1)} %bitcast.153, s32[1024]{0:T(1024)S(1)} %pad_clamp_fusion.1), kind=kCustom, calls=%fused_computation.clone | custom fusion | bytes 8390656 | tf_op jit(solution)/shard_map/jit(_take)/gather | solution.py:114
  161.4 3.4 %bitcast_select_fusion.1 = bf16[1,2,16,512,128]{4,2,1,3,0:T(8,128)(2,1)S(1)} fusion(bf16[512,2,16,128]{3,2,1,0:T(8,128)(2,1)} %gather_fusion, pred[512]{0:T(512)(128)(4,1)S(1)} %compare_and_fusion.1), kind=kLoop, calls=%fused_computation.91 | loop fusion | flops 2097152 | bytes 8389120 | tf_op jit(solution)/shard_map/jit(_take)/select_n | solution.py:114
  164.8 0.0 copy-done.2
  164.9 0.0 copy-done.6
  164.9 3.6 %fusion.20 = (bf16[1,16,512,128]{3,1,2,0:T(8,128)(2,1)S(1)}, bf16[1,16,512,128]{3,1,2,0:T(8,128)(2,1)S(1)}) fusion(f32[16,512]{0,1:T(8,128)S(1)} %copy-done.6, f32[16,512]{0,1:T(8,128)S(1)} %copy.72, bf16[1,2,16,512,128]{4,2,3,1,0:T(8,128)(2,1)S(1)} %copy-done.2, bf16[1,2,16,512,128]{4,2,1,3,0:T(8,128)(2,1)S(1)} %bitcast_select_fusion.1), kind=kLoop, calls=%fused_computation.99 | loop fusion | flops 18874368 | bytes 12648448 | tf_op jit(solution)/shard_map/stack | solution.py:139
  168.5 0.4 pad_maximum_fusion
  168.9 2.7 %copy.76 = bf16[2,16,512,128]{3,1,0,2:T(8,128)(2,1)} copy(bf16[2,16,512,128]{3,1,2,0:T(8,128)(2,1)S(1)} %pad_maximum_fusion) | data formatting | bytes 8388608 | tf_op jit(solution)/shard_map/stack | solution.py:139
  171.7 5.8 %all-to-all-start.1 = ((bf16[2,16,512,128]{3,1,0,2:T(8,128)(2,1)}), bf16[2,16,512,128]{3,1,0,2:T(8,128)(2,1)}, u32[]{:S(2)}, u32[]{:S(2)}) async-start(bf16[2,16,512,128]{3,1,0,2:T(8,128)(2,1)} %copy.76), calls=%async_computation.1 | async-start | bytes 8388608 | tf_op jit(solution)/shard_map/all_to_all | solution.py:142
  177.5 18.2 %cosine_convert_fusion = (bf16[1,2048,512]{2,1,0:T(8,128)(2,1)S(1)}, bf16[1,2048,512]{2,1,0:T(8,128)(2,1)}) fusion(s32[512]{0:T(512)S(1)} %iota_add_fusion.2), kind=kLoop, calls=%fused_computation.93 | loop fusion | flops 17825792 | bytes 4196352 | tf_op jit(solution)/shard_map/convert.12
  195.7 34.5 %all-to-all-done.1 = bf16[2,16,512,128]{3,1,0,2:T(8,128)(2,1)} async-done(((bf16[2,16,512,128]{3,1,0,2:T(8,128)(2,1)}), bf16[2,16,512,128]{3,1,0,2:T(8,128)(2,1)}, u32[]{:S(2)}, u32[]{:S(2)}) %all-to-all-start.1) | async-done | bytes 4194336 | tf_op jit(solution)/shard_map/all_to_all | solution.py:142
  230.2 3.1 %copy.78 = bf16[2,128,16,4,128]{4,2,1,3,0:T(8,128)(2,1)S(1)} copy(bf16[2,128,16,4,128]{4,2,0,3,1:T(8,128)(2,1)} %bitcast.67) | data formatting | bytes 8388608 | tf_op jit(solution)/shard_map/all_to_all | solution.py:142
  233.3 0.0 copy-start.1
  233.3 3.3 %fusion.23 = f32[4,128,512]{2,1,0:T(8,128)} fusion(bf16[2,2048,4,128]{3,1,2,0:T(8,128)(2,1)S(1)} %bitcast.162, bf16[1,2048,512]{2,1,0:T(8,128)(2,1)S(1)} %copy-done.5, bf16[1,2048,512]{2,1,0:T(8,128)(2,1)S(1)} %get-tuple-element.53, f32[4]{0:T(128)S(1)} %convert_multiply_fusion.4), kind=kOutput, calls=%fused_computation.105 | convolution fusion | flops 2149842944 | bytes 9437200 | tf_op jit(solution)/shard_map/rkpc,rkl->pcl/dot_general | solution.py:146
  (48 shorter events, 0.2 us)
Async XLA Ops:
  0.0 26.2 %copy-start = (bf16[128,1,4096]{2,0,1:T(8,128)(2,1)S(1)}, bf16[128,1,4096]{2,0,1:T(8,128)(2,1)}, u32[]{:S(2)}) copy-start(bf16[128,1,4096]{2,0,1:T(8,128)(2,1)} %param.7) | copy-start | bytes 3145732
  49.1 1.0 copy-start.3
  50.1 7.5 %copy-start.7 = (f32[33,2048]{1,0:T(8,128)S(1)}, f32[33,2048]{1,0:T(8,128)}, u32[]{:S(2)}) copy-start(f32[33,2048]{1,0:T(8,128)} %param.8) | copy-start | bytes 811012
  50.1 9.0 %copy-start.21 = (s32[512,2]{0,1:T(2,128)S(1)}, s32[512,2]{0,1:T(2,128)}, u32[]{:S(2)}) copy-start(s32[512,2]{0,1:T(2,128)} %param.9) | copy-start | bytes 12292
  50.1 9.0 %copy-start.22 = (s32[128]{0:T(128)S(1)}, s32[128]{0:T(128)}, u32[]{:S(2)}) copy-start(s32[128]{0:T(128)} %param.11) | copy-start | bytes 1540
  50.4 11.1 %collective-permute-start = (bf16[1,2,2048,16]{2,3,1,0:T(8,128)(2,1)S(1)}, bf16[1,2,2048,16]{2,3,1,0:T(8,128)(2,1)S(1)}, u32[]{:S(2)}, u32[]{:S(2)}) collective-permute-start(bf16[1,2,2048,16]{2,3,1,0:T(8,128)(2,1)S(1)} %copy.61), channel_id=1, source_target_pairs={{0,1},{1,2},{2,3},{3,4},{4,5},{5,6},{6,7},{7,8},{8,9},{9,10},{10,1... | collective-permute-start | bytes 393224 | tf_op jit(solution)/shard_map/ppermute | solution.py:20
  55.3 8.8 %copy-start.4 = (bf16[4096,128]{1,0:T(8,128)(2,1)S(1)}, bf16[4096,128]{1,0:T(8,128)(2,1)}, u32[]{:S(2)}) copy-start(bf16[4096,128]{1,0:T(8,128)(2,1)} %copy-done.3) | copy-start | bytes 3145732
  55.3 7.5 %collective-permute-start.1 = (bf16[1,2,2048,16]{2,3,1,0:T(8,128)(2,1)S(1)}, bf16[1,2,2048,16]{2,3,1,0:T(8,128)(2,1)S(1)}, u32[]{:S(2)}, u32[]{:S(2)}) collective-permute-start(bf16[1,2,2048,16]{2,3,1,0:T(8,128)(2,1)S(1)} %copy.63), channel_id=1, source_target_pairs={{1,0},{2,1},{3,2},{4,3},{5,4},{6,5},{7,6},{8,7},{9,8},{10,9},{11,1... | collective-permute-start | bytes 393224 | tf_op jit(solution)/shard_map/ppermute | solution.py:22
  59.0 5.2 %copy-start.8 = (f32[1,2048]{1,0:T(1,128)S(1)}, f32[1,2048]{1,0:T(1,128)}, u32[]{:S(2)}) copy-start(f32[1,2048]{1,0:T(1,128)} %get-tuple-element.26) | copy-start | bytes 24580
  59.0 5.2 %copy-start.9 = (f32[1,2048]{1,0:T(1,128)S(1)}, f32[1,2048]{1,0:T(1,128)}, u32[]{:S(2)}) copy-start(f32[1,2048]{1,0:T(1,128)} %get-tuple-element.27) | copy-start | bytes 24580
  59.0 5.2 %copy-start.10 = (f32[1,2048]{1,0:T(1,128)S(1)}, f32[1,2048]{1,0:T(1,128)}, u32[]{:S(2)}) copy-start(f32[1,2048]{1,0:T(1,128)} %get-tuple-element.28) | copy-start | bytes 24580
  59.1 5.2 %copy-start.11 = (f32[1,2048]{1,0:T(1,128)S(1)}, f32[1,2048]{1,0:T(1,128)}, u32[]{:S(2)}) copy-start(f32[1,2048]{1,0:T(1,128)} %get-tuple-element.29) | copy-start | bytes 24580
  59.1 5.2 %copy-start.12 = (f32[1,2048]{1,0:T(1,128)S(1)}, f32[1,2048]{1,0:T(1,128)}, u32[]{:S(2)}) copy-start(f32[1,2048]{1,0:T(1,128)} %get-tuple-element.30) | copy-start | bytes 24580
  59.1 5.2 %copy-start.13 = (f32[1,2048]{1,0:T(1,128)S(1)}, f32[1,2048]{1,0:T(1,128)}, u32[]{:S(2)}) copy-start(f32[1,2048]{1,0:T(1,128)} %get-tuple-element.31) | copy-start | bytes 24580
  59.1 5.2 %copy-start.14 = (f32[1,2048]{1,0:T(1,128)S(1)}, f32[1,2048]{1,0:T(1,128)}, u32[]{:S(2)}) copy-start(f32[1,2048]{1,0:T(1,128)} %get-tuple-element.32) | copy-start | bytes 24580
  59.1 5.2 %copy-start.15 = (f32[1,2048]{1,0:T(1,128)S(1)}, f32[1,2048]{1,0:T(1,128)}, u32[]{:S(2)}) copy-start(f32[1,2048]{1,0:T(1,128)} %get-tuple-element.33) | copy-start | bytes 24580
  59.1 0.6 copy-start.17
  59.1 0.6 copy-start.19
  107.6 0.7 copy-start.16
  108.8 20.7 %copy-start.20 = (s32[512,1]{0,1:T(1,128)S(1)}, s32[512,1]{0,1:T(1,128)}, u32[]{:S(2)}) copy-start(s32[512,1]{0,1:T(1,128)} %copy-done.19) | copy-start | bytes 6148
  108.8 20.7 %copy-start.18 = (s32[512,1]{0,1:T(1,128)S(1)}, s32[512,1]{0,1:T(1,128)}, u32[]{:S(2)}) copy-start(s32[512,1]{0,1:T(1,128)} %copy-done.17) | copy-start | bytes 6148
  118.3 30.3 %all-to-all-start = ((bf16[1,2,2048,128]{3,1,0,2:T(2,128)(2,1)}), bf16[1,2,2048,128]{3,1,0,2:T(2,128)(2,1)S(1)}, u32[]{:S(2)}, u32[]{:S(2)}) async-start(bf16[1,2,2048,128]{3,1,0,2:T(2,128)(2,1)} %copy.67), calls=%async_computation | async-start | bytes 2097152 | tf_op jit(solution)/shard_map/all_to_all | solution.py:109
  161.4 3.4 %copy-start.2 = (bf16[1,2,16,512,128]{4,2,3,1,0:T(8,128)(2,1)S(1)}, bf16[1,2,16,512,128]{4,2,3,1,0:T(8,128)(2,1)}, u32[]{:S(2)}) copy-start(bf16[1,2,16,512,128]{4,2,3,1,0:T(8,128)(2,1)} %bitcast_select_fusion) | copy-start | bytes 12582916
  161.4 3.5 %copy-start.6 = (f32[16,512]{0,1:T(8,128)S(1)}, f32[16,512]{0,1:T(8,128)}, u32[]{:S(2)}) copy-start(f32[16,512]{0,1:T(8,128)} %copy.75) | copy-start | bytes 98308
  171.7 5.9 %copy-start.23 = (s32[4]{0:T(128)S(1)}, s32[4]{0:T(128)}, u32[]{:S(2)}) copy-start(s32[4]{0:T(128)} %param.10) | copy-start | bytes 52
  171.7 58.5 %all-to-all-start.1 = ((bf16[2,16,512,128]{3,1,0,2:T(8,128)(2,1)}), bf16[2,16,512,128]{3,1,0,2:T(8,128)(2,1)}, u32[]{:S(2)}, u32[]{:S(2)}) async-start(bf16[2,16,512,128]{3,1,0,2:T(8,128)(2,1)} %copy.76), calls=%async_computation.1 | async-start | bytes 8388608 | tf_op jit(solution)/shard_map/all_to_all | solution.py:142
  230.2 3.1 %copy-start.5 = (bf16[1,2048,512]{2,1,0:T(8,128)(2,1)S(1)}, bf16[1,2048,512]{2,1,0:T(8,128)(2,1)}, u32[]{:S(2)}) copy-start(bf16[1,2048,512]{2,1,0:T(8,128)(2,1)} %get-tuple-element.54) | copy-start | bytes 6291460
  233.3 3.4 %copy-start.1 = (bf16[128,1,4096]{2,0,1:T(8,128)(2,1)S(1)}, bf16[128,1,4096]{2,0,1:T(8,128)(2,1)}, u32[]{:S(2)}) copy-start(bf16[128,1,4096]{2,0,1:T(8,128)(2,1)} %param.7) | copy-start | bytes 3145732
where the time goes:
time: 237 us
  other arithmetic  101 us (43%)
  waiting for transfers between devices  53.4 us (23%)
  local copies, waits for them, and re-layouts  31.9 us (13%)
  matrix products  26.3 us (11%)
  starting transfers between devices  23.9 us (10%)
    add x1, other arithmetic, whiten(): filtered + fan_taps[offset][None, None, :, None] * padded[:, :, :, offset...  40 us
    all_to_all x1, waiting for transfers between devices, body(): lax.all_to_all(cross_spec, ('group', 'shard'), split_axis=2, concat_axis=...  34.5 us
    dot_general x1, matrix products, body(): jnp.einsum('cst,tk->skc', samples, forward, preferred_element_type=jnp.fl...  22.9 us
    sub x1, other arithmetic, forward_tables(): cosine = (cos_a * cos_b - sin_a * sin_b).reshape(length, bin_count)  22 us
    another operation x4, other arithmetic  20.1 us
    all_to_all x1, waiting for transfers between devices, body(): lax.all_to_all(whitened, ('group', 'shard'), split_axis=2, concat_axis=3,...  19 us
    all_to_all x1, starting transfers between devices, body(): lax.all_to_all(whitened, ('group', 'shard'), split_axis=2, concat_axis=3,...  11.2 us
    convert_element_type x1, local copies, waits for them, and re-layouts, whiten(): (filtered * lax.rsqrt(mean_power + EPSILON)[:, None]).astype(jnp.bfloat16)  9.46 us
  transfers between devices with their start and end apart: 4, of which 2 were waited for; matrix products, arithmetic and copies ran while one was open for 10% of the time, Pallas kernels for 0%

commit v1 on v0

--- a/solution.py
+++ b/solution.py
@@ -106,7 +106,10 @@
         HALF,
     )
     whitened = whiten(padded, fan_taps)
-    banded = lax.all_to_all(whitened, ("group", "shard"), split_axis=2, concat_axis=3, tiled=True)
+    size = lax.axis_size(("group", "shard"))
+    tiles = jnp.stack(jnp.split(whitened, size, axis=2), axis=0)
+    tiles = lax.all_to_all(tiles, ("group", "shard"), split_axis=0, concat_axis=0)
+    banded = jnp.concatenate(tiles, axis=3)
     first_block = pair_blocks[:, 0]
     second_block = pair_blocks[:, 1]
     blocks = banded.reshape(segments, 2, bins_device, devices, block_width)

time: 237 us -> 305 us (1.29)
  local copies, waits for them, and re-layouts: 31.9 us -> 99.2 us
    unnamed x48 -> x175, local copies, waits for them, and re-layouts: 1.42 us -> 77.6 us
    convert_element_type x1 -> x0, local copies, waits for them, and re-layouts: 9.46 us -> none  [whiten(): (filtered * lax.rsqrt(mean_power + EPSILON)[:, None]).astype(jnp.bfloat16)]
  transfers between devices with their start and end apart: 4 -> 4, of which waited for: 2 -> 2; matrix products, arithmetic and copies ran while one was open for 10% -> 8% of each run, Pallas kernels for 0% -> 0%
where the time goes in v1:
time: 305 us; the launch traced here: 304 us
  other arithmetic  101 us (33%)
  local copies, waits for them, and re-layouts  99.2 us (33%)
  waiting for transfers between devices  53.4 us (18%)
  matrix products  26.3 us (9%)
  starting transfers between devices  23.9 us (8%)
    unnamed x175, local copies, waits for them, and re-layouts  77.6 us
    add x1, other arithmetic, whiten(): filtered + fan_taps[offset][None, None, :, None] * padded[:, :, :, offset...  40 us
    all_to_all x1, waiting for transfers between devices, body(): lax.all_to_all(cross_spec, ('group', 'shard'), split_axis=2, concat_axis=...  34.5 us
    dot_general x1, matrix products, body(): jnp.einsum('cst,tk->skc', samples, forward, preferred_element_type=jnp.fl...  22.9 us
    sub x1, other arithmetic, forward_tables(): cosine = (cos_a * cos_b - sin_a * sin_b).reshape(length, bin_count)  22 us
    another operation x4, other arithmetic  20.1 us
    all_to_all x1, waiting for transfers between devices, body(): lax.all_to_all(tiles, ('group', 'shard'), split_axis=0, concat_axis=0)  19 us
    all_to_all x1, starting transfers between devices, body(): lax.all_to_all(tiles, ('group', 'shard'), split_axis=0, concat_axis=0)  11.2 us
  transfers between devices with their start and end apart: 4, of which 2 were waited for; matrix products, arithmetic and copies ran while one was open for 8% of the time, Pallas kernels for 0%

profile of v1, /device:TPU:1, one launch (start us, length us, event | category | flops | bytes accessed | tf_op | source)
XLA Modules:
  0.0 304.1 jit_solution(13316119830047584969)
XLA Ops:
  0.0 2.0 fusion.74
  2.1 2.1 fusion.77
  4.2 22.0 %multiply_subtract_fusion = (f32[64,64,2048]{2,1,0:T(8,128)}, f32[64,64,2048]{2,1,0:T(8,128)}) fusion(f32[64,2048]{1,0:T(8,128)S(1)} %get-tuple-element.59, f32[64,2048]{1,0:T(8,128)S(1)} %get-tuple-element.58, f32[64,2048]{1,0:T(8,128)S(1)} %get-tuple-element.60, f32[64,2048]{1,0:T(8,128)S(1)} %get-tuple-element.57), kind=kLoop, calls=%fused_computation.5 | loop fusion | flops 58720256 | bytes 69206016 | tf_op jit(solution)/shard_map/sub | solution.py:40
  26.2 22.9 %fusion.3 = bf16[4096,128]{1,0:T(8,128)(2,1)S(1)} fusion(f32[4096,2048]{1,0:T(8,128)} %bitcast.668, f32[4096,2048]{1,0:T(8,128)} %bitcast.667, bf16[128,1,4096]{2,0,1:T(8,128)(2,1)S(1)} %copy-done), kind=kOutput, calls=%fused_computation.76 | convolution fusion | flops 4345823232 | bytes 69206016 | tf_op jit(solution)/shard_map/cst,tk->skc/dot_general | solution.py:102
  50.4 4.6 %collective-permute-start = (bf16[1,2,2048,16]{2,3,1,0:T(8,128)(2,1)S(1)}, bf16[1,2,2048,16]{2,3,1,0:T(8,128)(2,1)S(1)}, u32[]{:S(2)}, u32[]{:S(2)}) collective-permute-start(bf16[1,2,2048,16]{2,3,1,0:T(8,128)(2,1)S(1)} %copy.328), channel_id=1, source_target_pairs={{0,1},{1,2},{2,3},{3,4},{4,5},{5,6},{6,7},{7,8},{8,9},{9,10},{10,1... | collective-permute-start | bytes 393224 | tf_op jit(solution)/shard_map/ppermute | solution.py:20
  55.3 2.2 collective-permute-start.1
  57.6 0.7 fusion.93
  58.3 0.7 fusion.94
  60.1 0.9 copy.341
  60.9 0.6 fusion.86
  61.5 1.3 copy.329
  62.9 1.3 copy.331
  64.3 40.0 %multiply_add_fusion = f32[1,2,2048,128]{3,2,1,0:T(8,128)S(1)} fusion(bf16[1,2,2048,128]{3,2,1,0:T(8,128)(2,1)S(1)} %bitcast.670, bf16[1,2,2048,16]{3,2,1,0:T(8,128)(2,1)} %copy.331, bf16[1,2,2048,16]{3,2,1,0:T(8,128)(2,1)} %copy.329, f32[2048]{0:T(1024)} %bitcast.707, f32[2048]{0:T(1024)} %bitcast.708, f32[2048]{0:T(1024)S(1)} %bitcast.677, ...), kind=kLoop, calls=%fused_computation.103 | loop fusion | flops 101711872 | bytes 3678208 | tf_op jit(solution)/shard_map/add | solution.py:84
  104.3 0.6 fusion.60
  105.0 1.3 copy.333
  106.3 1.3 bitcast_add_fusion
  108.9 0.6 constant_dynamic-update-slice_fusion.127
  109.5 0.6 constant_dynamic-update-slice_fusion.126
  110.1 0.6 constant_dynamic-update-slice_fusion.125
  110.7 0.6 constant_dynamic-update-slice_fusion.124
  111.3 0.6 constant_dynamic-update-slice_fusion.123
  111.9 0.6 constant_dynamic-update-slice_fusion.122
  112.5 0.6 constant_dynamic-update-slice_fusion.121
  113.1 0.6 constant_dynamic-update-slice_fusion.120
  113.7 0.6 constant_dynamic-update-slice_fusion.119
  114.3 0.6 constant_dynamic-update-slice_fusion.118
  114.9 0.6 constant_dynamic-update-slice_fusion.117
  115.5 0.6 constant_dynamic-update-slice_fusion.116
  116.1 0.6 constant_dynamic-update-slice_fusion.115
  116.7 0.6 constant_dynamic-update-slice_fusion.114
  117.3 0.6 constant_dynamic-update-slice_fusion.113
  117.9 0.6 constant_dynamic-update-slice_fusion.112
  118.5 0.6 constant_dynamic-update-slice_fusion.111
  119.1 0.6 constant_dynamic-update-slice_fusion.110
  119.7 0.6 constant_dynamic-update-slice_fusion.109
  120.3 0.6 constant_dynamic-update-slice_fusion.108
  120.9 0.6 constant_dynamic-update-slice_fusion.107
  121.5 0.6 constant_dynamic-update-slice_fusion.106
  122.1 0.6 constant_dynamic-update-slice_fusion.105
  122.7 0.6 constant_dynamic-update-slice_fusion.104
  123.3 0.6 constant_dynamic-update-slice_fusion.103
  123.9 0.6 constant_dynamic-update-slice_fusion.102
  124.5 0.6 constant_dynamic-update-slice_fusion.101
  125.1 0.6 constant_dynamic-update-slice_fusion.100
  125.7 0.6 constant_dynamic-update-slice_fusion.99
  126.3 0.6 constant_dynamic-update-slice_fusion.98
  126.9 0.6 constant_dynamic-update-slice_fusion.97
  127.5 0.6 constant_dynamic-update-slice_fusion.96
  128.1 0.6 constant_dynamic-update-slice_fusion.95
  128.7 0.6 constant_dynamic-update-slice_fusion.94
  129.3 0.6 constant_dynamic-update-slice_fusion.93
  185.7 11.2 %all-to-all-start = ((bf16[128,1,2,16,128]{4,3,2,1,0:T(8,128)(2,1)}), bf16[128,1,2,16,128]{4,3,2,1,0:T(8,128)(2,1)S(1)}, u32[]{:S(2)}, u32[]{:S(2)}) async-start(bf16[128,1,2,16,128]{4,3,2,1,0:T(8,128)(2,1)} %constant_dynamic-update-slice_fusion), calls=%async_computation | async-start | bytes 2097152 | tf_op jit(solution)/shard_map/all_to_all | solution.py:111
  197.0 19.0 %all-to-all-done = bf16[128,1,2,16,128]{4,3,2,1,0:T(8,128)(2,1)S(1)} async-done(((bf16[128,1,2,16,128]{4,3,2,1,0:T(8,128)(2,1)}), bf16[128,1,2,16,128]{4,3,2,1,0:T(8,128)(2,1)S(1)}, u32[]{:S(2)}, u32[]{:S(2)}) %all-to-all-start) | async-done | bytes 1048608 | tf_op jit(solution)/shard_map/all_to_all | solution.py:111
  217.3 3.5 %gather_fusion.1 = bf16[512,2,16,128]{3,2,1,0:T(8,128)(2,1)} fusion(bf16[2,16,128,128]{3,1,2,0:T(8,128)(2,1)S(1)} %maximum_bitcast_fusion.6, s32[1024]{0:T(1024)S(1)} %pad_clamp_fusion), kind=kCustom, calls=%fused_computation.1.clone | custom fusion | bytes 8390656 | tf_op jit(solution)/shard_map/jit(_take)/gather | solution.py:118
  220.8 4.6 %bitcast_select_fusion = bf16[1,2,16,512,128]{4,2,3,1,0:T(8,128)(2,1)} fusion(bf16[512,2,16,128]{3,2,1,0:T(8,128)(2,1)} %gather_fusion.1, pred[512]{0:T(512)(128)(4,1)S(1)} %compare_and_fusion), kind=kLoop, calls=%fused_computation.90 | loop fusion | flops 2097152 | bytes 8389120 | tf_op jit(solution)/shard_map/jit(_take)/select_n | solution.py:118
  225.3 3.5 %gather_fusion = bf16[512,2,16,128]{3,2,1,0:T(8,128)(2,1)} fusion(bf16[2,16,128,128]{3,1,2,0:T(8,128)(2,1)S(1)} %bitcast.666, s32[1024]{0:T(1024)S(1)} %pad_clamp_fusion.1), kind=kCustom, calls=%fused_computation.clone | custom fusion | bytes 8390656 | tf_op jit(solution)/shard_map/jit(_take)/gather | solution.py:117
  228.9 3.4 %bitcast_select_fusion.1 = bf16[1,2,16,512,128]{4,2,1,3,0:T(8,128)(2,1)S(1)} fusion(bf16[512,2,16,128]{3,2,1,0:T(8,128)(2,1)} %gather_fusion, pred[512]{0:T(512)(128)(4,1)S(1)} %compare_and_fusion.1), kind=kLoop, calls=%fused_computation.91 | loop fusion | flops 2097152 | bytes 8389120 | tf_op jit(solution)/shard_map/jit(_take)/select_n | solution.py:117
  232.3 3.6 %fusion.20 = (bf16[1,16,512,128]{3,1,2,0:T(8,128)(2,1)S(1)}, bf16[1,16,512,128]{3,1,2,0:T(8,128)(2,1)S(1)}) fusion(f32[16,512]{0,1:T(8,128)S(1)} %copy-done.6, f32[16,512]{0,1:T(8,128)S(1)} %copy.338, bf16[1,2,16,512,128]{4,2,3,1,0:T(8,128)(2,1)S(1)} %copy-done.2, bf16[1,2,16,512,128]{4,2,1,3,0:T(8,128)(2,1)S(1)} %bitcast_select_fusion.1), kind=kLoop, calls=%fused_computation.99 | loop fusion | flops 18874368 | bytes 12648448 | tf_op jit(solution)/shard_map/stack | solution.py:142
  236.3 2.7 copy.342
  239.1 5.8 %all-to-all-start.1 = ((bf16[2,16,512,128]{3,1,0,2:T(8,128)(2,1)}), bf16[2,16,512,128]{3,1,0,2:T(8,128)(2,1)}, u32[]{:S(2)}, u32[]{:S(2)}) async-start(bf16[2,16,512,128]{3,1,0,2:T(8,128)(2,1)} %copy.342), calls=%async_computation.1 | async-start | bytes 8388608 | tf_op jit(solution)/shard_map/all_to_all | solution.py:145
  245.0 18.2 %cosine_convert_fusion = (bf16[1,2048,512]{2,1,0:T(8,128)(2,1)S(1)}, bf16[1,2048,512]{2,1,0:T(8,128)(2,1)}) fusion(s32[512]{0:T(512)S(1)} %iota_add_fusion.2), kind=kLoop, calls=%fused_computation.93 | loop fusion | flops 17825792 | bytes 4196352 | tf_op jit(solution)/shard_map/convert.12
  263.2 34.5 %all-to-all-done.1 = bf16[2,16,512,128]{3,1,0,2:T(8,128)(2,1)} async-done(((bf16[2,16,512,128]{3,1,0,2:T(8,128)(2,1)}), bf16[2,16,512,128]{3,1,0,2:T(8,128)(2,1)}, u32[]{:S(2)}, u32[]{:S(2)}) %all-to-all-start.1) | async-done | bytes 4194336 | tf_op jit(solution)/shard_map/all_to_all | solution.py:145
  297.6 3.1 %copy.344 = bf16[2,128,16,4,128]{4,2,1,3,0:T(8,128)(2,1)S(1)} copy(bf16[2,128,16,4,128]{4,2,0,3,1:T(8,128)(2,1)} %bitcast.193) | data formatting | bytes 8388608 | tf_op jit(solution)/shard_map/all_to_all | solution.py:145
  300.8 3.3 %fusion.23 = f32[4,128,512]{2,1,0:T(8,128)} fusion(bf16[2,2048,4,128]{3,1,2,0:T(8,128)(2,1)S(1)} %bitcast.675, bf16[1,2048,512]{2,1,0:T(8,128)(2,1)S(1)} %copy-done.5, bf16[1,2048,512]{2,1,0:T(8,128)(2,1)S(1)} %get-tuple-element.55, f32[4]{0:T(128)S(1)} %convert_multiply_fusion.4), kind=kOutput, calls=%fused_computation.105 | convolution fusion | flops 2149842944 | bytes 9437200 | tf_op jit(solution)/shard_map/rkpc,rkl->pcl/dot_general | solution.py:149
  (175 shorter events, 61.5 us)
Async XLA Ops:
  0.0 26.2 %copy-start = (bf16[128,1,4096]{2,0,1:T(8,128)(2,1)S(1)}, bf16[128,1,4096]{2,0,1:T(8,128)(2,1)}, u32[]{:S(2)}) copy-start(bf16[128,1,4096]{2,0,1:T(8,128)(2,1)} %param.7) | copy-start | bytes 3145732
  49.1 1.0 copy-start.3
  50.1 7.5 %copy-start.7 = (f32[33,2048]{1,0:T(8,128)S(1)}, f32[33,2048]{1,0:T(8,128)}, u32[]{:S(2)}) copy-start(f32[33,2048]{1,0:T(8,128)} %param.8) | copy-start | bytes 811012
  50.1 9.0 %copy-start.21 = (s32[512,2]{0,1:T(2,128)S(1)}, s32[512,2]{0,1:T(2,128)}, u32[]{:S(2)}) copy-start(s32[512,2]{0,1:T(2,128)} %param.9) | copy-start | bytes 12292
  50.1 9.0 %copy-start.22 = (s32[128]{0:T(128)S(1)}, s32[128]{0:T(128)}, u32[]{:S(2)}) copy-start(s32[128]{0:T(128)} %param.11) | copy-start | bytes 1540
  50.4 11.1 %collective-permute-start = (bf16[1,2,2048,16]{2,3,1,0:T(8,128)(2,1)S(1)}, bf16[1,2,2048,16]{2,3,1,0:T(8,128)(2,1)S(1)}, u32[]{:S(2)}, u32[]{:S(2)}) collective-permute-start(bf16[1,2,2048,16]{2,3,1,0:T(8,128)(2,1)S(1)} %copy.328), channel_id=1, source_target_pairs={{0,1},{1,2},{2,3},{3,4},{4,5},{5,6},{6,7},{7,8},{8,9},{9,10},{10,1... | collective-permute-start | bytes 393224 | tf_op jit(solution)/shard_map/ppermute | solution.py:20
  55.3 8.8 %copy-start.4 = (bf16[4096,128]{1,0:T(8,128)(2,1)S(1)}, bf16[4096,128]{1,0:T(8,128)(2,1)}, u32[]{:S(2)}) copy-start(bf16[4096,128]{1,0:T(8,128)(2,1)} %copy-done.3) | copy-start | bytes 3145732
  55.3 7.5 %collective-permute-start.1 = (bf16[1,2,2048,16]{2,3,1,0:T(8,128)(2,1)S(1)}, bf16[1,2,2048,16]{2,3,1,0:T(8,128)(2,1)S(1)}, u32[]{:S(2)}, u32[]{:S(2)}) collective-permute-start(bf16[1,2,2048,16]{2,3,1,0:T(8,128)(2,1)S(1)} %copy.330), channel_id=1, source_target_pairs={{1,0},{2,1},{3,2},{4,3},{5,4},{6,5},{7,6},{8,7},{9,8},{10,9},{11,1... | collective-permute-start | bytes 393224 | tf_op jit(solution)/shard_map/ppermute | solution.py:22
  59.0 5.2 %copy-start.8 = (f32[1,2048]{1,0:T(1,128)S(1)}, f32[1,2048]{1,0:T(1,128)}, u32[]{:S(2)}) copy-start(f32[1,2048]{1,0:T(1,128)} %get-tuple-element.28) | copy-start | bytes 24580
  59.0 5.2 %copy-start.9 = (f32[1,2048]{1,0:T(1,128)S(1)}, f32[1,2048]{1,0:T(1,128)}, u32[]{:S(2)}) copy-start(f32[1,2048]{1,0:T(1,128)} %get-tuple-element.29) | copy-start | bytes 24580
  59.0 5.2 %copy-start.10 = (f32[1,2048]{1,0:T(1,128)S(1)}, f32[1,2048]{1,0:T(1,128)}, u32[]{:S(2)}) copy-start(f32[1,2048]{1,0:T(1,128)} %get-tuple-element.30) | copy-start | bytes 24580
  59.1 5.2 %copy-start.11 = (f32[1,2048]{1,0:T(1,128)S(1)}, f32[1,2048]{1,0:T(1,128)}, u32[]{:S(2)}) copy-start(f32[1,2048]{1,0:T(1,128)} %get-tuple-element.31) | copy-start | bytes 24580
  59.1 5.2 %copy-start.12 = (f32[1,2048]{1,0:T(1,128)S(1)}, f32[1,2048]{1,0:T(1,128)}, u32[]{:S(2)}) copy-start(f32[1,2048]{1,0:T(1,128)} %get-tuple-element.32) | copy-start | bytes 24580
  59.1 5.2 %copy-start.13 = (f32[1,2048]{1,0:T(1,128)S(1)}, f32[1,2048]{1,0:T(1,128)}, u32[]{:S(2)}) copy-start(f32[1,2048]{1,0:T(1,128)} %get-tuple-element.33) | copy-start | bytes 24580
  59.1 5.2 %copy-start.14 = (f32[1,2048]{1,0:T(1,128)S(1)}, f32[1,2048]{1,0:T(1,128)}, u32[]{:S(2)}) copy-start(f32[1,2048]{1,0:T(1,128)} %get-tuple-element.34) | copy-start | bytes 24580
  59.1 5.2 %copy-start.15 = (f32[1,2048]{1,0:T(1,128)S(1)}, f32[1,2048]{1,0:T(1,128)}, u32[]{:S(2)}) copy-start(f32[1,2048]{1,0:T(1,128)} %get-tuple-element.35) | copy-start | bytes 24580
  59.1 0.6 copy-start.17
  59.1 0.6 copy-start.19
  107.6 0.7 copy-start.16
  108.9 88.0 %copy-start.20 = (s32[512,1]{0,1:T(1,128)S(1)}, s32[512,1]{0,1:T(1,128)}, u32[]{:S(2)}) copy-start(s32[512,1]{0,1:T(1,128)} %copy-done.19) | copy-start | bytes 6148
  109.5 87.5 %copy-start.18 = (s32[512,1]{0,1:T(1,128)S(1)}, s32[512,1]{0,1:T(1,128)}, u32[]{:S(2)}) copy-start(s32[512,1]{0,1:T(1,128)} %copy-done.17) | copy-start | bytes 6148
  185.7 30.3 %all-to-all-start = ((bf16[128,1,2,16,128]{4,3,2,1,0:T(8,128)(2,1)}), bf16[128,1,2,16,128]{4,3,2,1,0:T(8,128)(2,1)S(1)}, u32[]{:S(2)}, u32[]{:S(2)}) async-start(bf16[128,1,2,16,128]{4,3,2,1,0:T(8,128)(2,1)} %constant_dynamic-update-slice_fusion), calls=%async_computation | async-start | bytes 2097152 | tf_op jit(solution)/shard_map/all_to_all | solution.py:111
  228.9 3.4 %copy-start.2 = (bf16[1,2,16,512,128]{4,2,3,1,0:T(8,128)(2,1)S(1)}, bf16[1,2,16,512,128]{4,2,3,1,0:T(8,128)(2,1)}, u32[]{:S(2)}) copy-start(bf16[1,2,16,512,128]{4,2,3,1,0:T(8,128)(2,1)} %bitcast_select_fusion) | copy-start | bytes 12582916
  228.9 3.5 %copy-start.6 = (f32[16,512]{0,1:T(8,128)S(1)}, f32[16,512]{0,1:T(8,128)}, u32[]{:S(2)}) copy-start(f32[16,512]{0,1:T(8,128)} %copy.341) | copy-start | bytes 98308
  239.1 5.9 %copy-start.23 = (s32[4]{0:T(128)S(1)}, s32[4]{0:T(128)}, u32[]{:S(2)}) copy-start(s32[4]{0:T(128)} %param.10) | copy-start | bytes 52
  239.1 58.5 %all-to-all-start.1 = ((bf16[2,16,512,128]{3,1,0,2:T(8,128)(2,1)}), bf16[2,16,512,128]{3,1,0,2:T(8,128)(2,1)}, u32[]{:S(2)}, u32[]{:S(2)}) async-start(bf16[2,16,512,128]{3,1,0,2:T(8,128)(2,1)} %copy.342), calls=%async_computation.1 | async-start | bytes 8388608 | tf_op jit(solution)/shard_map/all_to_all | solution.py:145
  297.6 3.1 %copy-start.5 = (bf16[1,2048,512]{2,1,0:T(8,128)(2,1)S(1)}, bf16[1,2048,512]{2,1,0:T(8,128)(2,1)}, u32[]{:S(2)}) copy-start(bf16[1,2048,512]{2,1,0:T(8,128)(2,1)} %get-tuple-element.56) | copy-start | bytes 6291460
  300.7 3.4 %copy-start.1 = (bf16[128,1,4096]{2,0,1:T(8,128)(2,1)S(1)}, bf16[128,1,4096]{2,0,1:T(8,128)(2,1)}, u32[]{:S(2)}) copy-start(bf16[128,1,4096]{2,0,1:T(8,128)(2,1)} %param.7) | copy-start | bytes 3145732
